TPU v7x, 32 devices: a whole 2x2x4 slice. The times are simulated.
32 devices in a mesh: grp: 2 (over x), tm: 16 (over z, y, core).
Axes of the slice: x: 2, y: 2, z: 4, core: 2. Of those that a mesh axis runs over, the one named last changes fastest.
Arguments:
- frames_in: bfloat16 [16384, 1536], P(('grp', 'tm')), parts along dimension 0, may hold values from -6 to 6
- frame_time: int32 [64], P('grp'), parts along dimension 0, may hold values from 0 to 31, each once
- norm_gain: float32 [1536], replicated, may hold values from 0.25 to 1.75
- w_query: bfloat16 [1536, 768], replicated, may hold values from -2 to 2
- w_key: bfloat16 [1536, 768], replicated, may hold values from -2 to 2
- w_value: bfloat16 [1536, 768], replicated, may hold values from -0.15625 to 0.15625
- w_output: bfloat16 [768, 1536], replicated, may hold values from -0.21875 to 0.21875
Outputs:
- attended: bfloat16 [16384, 1536], P(('grp', 'tm')), parts along dimension 0
There are 2 independent parts, one for each index of `grp`. A program takes and returns all parts, laid end to end along the dimension named above; an argument that names none is the same for every part. Nothing has to cross between parts.
Inputs may be any that keep to these rules, and one draw needn't show every extreme that they name: `frame_time`: each of 0 to 31 stands once.
All inputs are finite; a program needn't handle non-finite values.
Results may differ from a plain program's by a relative error of at most 0.004.
The roundings to bfloat16 on the way count: a program that leaves them out, or rounds other values in their place, can miss the bound.
Values may be sent and summed in bfloat16 or wider, within the bound.
A program may use at most 128 MiB of HBM per device.

v0:
```python
import jax
import jax.numpy as jnp
from jax import lax
from jax.sharding import PartitionSpec as P

HEADS = 6
HD = 128
HH = 16
WW = 16
WIN = 8
POOL = 4


def normed_rows(frames_in, norm_gain):
    values_f = frames_in.astype(jnp.float32)
    scale = lax.rsqrt(jnp.mean(values_f * values_f, axis=-1, keepdims=True) + 1e-06)
    return (values_f * scale * norm_gain).astype(jnp.bfloat16)


def to_windows(array, count):
    shaped = array.reshape(count, HH // WIN, WIN, WW // WIN, WIN, HEADS, HD)
    shaped = shaped.transpose(0, 1, 3, 2, 4, 5, 6)
    return shaped.reshape(count, HH // WIN * (WW // WIN), WIN * WIN, HEADS, HD)


def from_windows(array, count):
    shaped = array.reshape(count, HH // WIN, WW // WIN, WIN, WIN, HEADS * HD)
    shaped = shaped.transpose(0, 1, 3, 2, 4, 5)
    return shaped.reshape(count * HH * WW, HEADS * HD)


def pooled(array, count):
    pool_rows = HH // POOL * (WW // POOL)
    shaped = array.reshape(count, HH // POOL, POOL, WW // POOL, POOL, HEADS * HD).astype(
        jnp.float32
    )
    return jnp.mean(shaped, axis=(2, 4)).reshape(count * pool_rows, HEADS * HD).astype(jnp.bfloat16)


def on_device(frames_in, frame_time, norm_gain, w_query, w_key, w_value, w_output):
    count = frames_in.shape[0] // (HH * WW)
    pool_rows = HH // POOL * (WW // POOL)
    all_frames = frame_time.shape[0]
    normed = normed_rows(frames_in, norm_gain)
    query = jnp.dot(normed, w_query, preferred_element_type=jnp.float32).astype(jnp.bfloat16)
    keys = jnp.dot(normed, w_key, preferred_element_type=jnp.float32).astype(jnp.bfloat16)
    values = jnp.dot(normed, w_value, preferred_element_type=jnp.float32).astype(jnp.bfloat16)
    pooled_keys = pooled(keys, count)
    pooled_values = pooled(values, count)
    own_time = lax.dynamic_slice_in_dim(frame_time, lax.axis_index("tm") * count, count)
    query_win = to_windows(query, count)
    factor = 1.0 / HD**0.5
    local_s = (
        jnp.einsum(
            "fnqhd,fnkhd->fnhqk",
            query_win,
            to_windows(keys, count),
            preferred_element_type=jnp.float32,
        )
        * factor
    )
    top = jnp.max(local_s, -1)
    local_w = jnp.exp(local_s - top[..., None])
    local_acc = jnp.einsum(
        "fnhqk,fnkhd->fnhqd",
        local_w.astype(jnp.bfloat16),
        to_windows(values, count),
        preferred_element_type=jnp.float32,
    )
    whole_keys, whole_values = (
        lax.all_gather(pooled_keys, "tm", axis=0, tiled=True),
        lax.all_gather(pooled_values, "tm", axis=0, tiled=True),
    )
    rows = whole_keys.shape[0]
    slot = jnp.arange(rows, dtype=jnp.int32) // pool_rows
    match = slot[:, None] == jnp.arange(all_frames, dtype=jnp.int32)[None, :]
    key_time = jnp.sum(jnp.where(match, frame_time[None, :], 0), axis=1)
    best = top
    total = jnp.sum(local_w, -1)
    acc = local_acc
    scores = (
        jnp.einsum(
            "fnqhd,khd->fnhqk",
            query_win,
            whole_keys.reshape(rows, HEADS, HD),
            preferred_element_type=jnp.float32,
        )
        * factor
    )
    valid = (key_time[None, :] < own_time[:, None])[:, None, None, None, :]
    scores = jnp.where(valid, scores, -1e30)
    new_best = jnp.maximum(best, jnp.max(scores, -1))
    keep = jnp.exp(best - new_best)
    weights = jnp.where(valid, jnp.exp(scores - new_best[..., None]), 0.0)
    total = total * keep + jnp.sum(weights, -1)
    acc = acc * keep[..., None] + jnp.einsum(
        "fnhqk,khd->fnhqd",
        weights.astype(jnp.bfloat16),
        whole_values.reshape(rows, HEADS, HD),
        preferred_element_type=jnp.float32,
    )
    final = (new_best, total, acc)
    best, total, acc = final
    mixed = (acc / total[..., None]).transpose(0, 1, 3, 2, 4).astype(jnp.bfloat16)
    mixed = from_windows(mixed, count)
    return jnp.dot(mixed, w_output, preferred_element_type=jnp.float32).astype(jnp.bfloat16)


def solution(mesh):
    placed = (P(("grp", "tm"), None), P("grp"), P(), P(), P(), P(), P())
    return jax.shard_map(
        on_device, mesh=mesh, in_specs=placed, out_specs=P(("grp", "tm"), None), check_vma=False
    )
```

profile of v0, /device:TPU:0, one launch (start us, length us, event | category | flops | bytes accessed | tf_op | source)
XLA Modules:
  0.0 85.4 jit_solution(2821864571280386767)
XLA Ops:
  0.0 0.0 copy-start
  0.0 0.9 %dynamic_slice.3 = s32[2]{0:T(128)S(1)} dynamic-slice(s32[32]{0:T(128)} %param.8, s32[]{:T(128)S(6)} %select_n.25), dynamic_slice_sizes={2} | dynamic-slice | bytes 20 | tf_op jit(solution)/shard_map/dynamic_slice | solution.py:50
  0.9 0.7 select_reduce_fusion
  1.6 0.1 broadcast_compare_fusion
  1.7 1.8 %fusion.3 = f32[512]{0:T(512)S(1)} fusion(bf16[512,1536]{1,0:T(8,128)(2,1)} %param.7), kind=kLoop, calls=%fused_computation.7 | loop fusion | flops 2358784 | bytes 1574912 | tf_op jit(solution)/shard_map/reduce_sum | solution.py:16
  3.5 3.6 %convolution_convert_fusion.2 = bf16[512,768]{1,0:T(8,128)(2,1)S(1)} fusion(bf16[1536,768]{1,0:T(8,128)(2,1)} %param.11, bf16[512,1536]{1,0:T(8,128)(2,1)} %param.7, f32[1536]{0:T(1024)} %param.9, f32[512]{0:T(512)S(1)} %add_rsqrt_fusion), kind=kOutput, calls=%fused_computation.20 | convolution fusion | flops 1211498496 | bytes 4726784 | tf_op jit(solution)/shard_map/dot_general | solution.py:46
  7.1 0.0 copy-start.3
  7.1 1.5 %reshape.124 = f32[2,4,4,4,4,768]{5,4,3,2,1,0:T(4,128)} reshape(bf16[512,768]{1,0:T(8,128)(2,1)S(1)} %convolution_convert_fusion.2) | data formatting | bytes 2359296 | tf_op jit(solution)/shard_map/convert_element_type | solution.py:34
  8.6 0.0 copy-start.9
  8.6 1.9 %reduce_sum.60 = f32[2,4,4,768]{3,2,1,0:T(4,128)S(1)} reduce(f32[2,4,4,4,4,768]{5,4,3,2,1,0:T(4,128)} %reshape.124, f32[]{:T(128)} %constant.15.clone.1), dimensions={2,4}, to_apply=%region_3.0 | reduce | flops 368640 | bytes 1671172 | tf_op jit(solution)/shard_map/reduce_sum | solution.py:37
  10.6 0.0 copy-done.3
  10.6 26.7 %all_gather.6 = bf16[512,768]{1,0:T(8,128)(2,1)} all-gather(bf16[32,768]{1,0:T(8,128)(2,1)S(1)} %convert_element_type.60), channel_id=1, replica_groups=mesh['grp'=2,'tm'=16] {'tm'}, dimensions={0}, use_global_device_ids=true | all-gather | bytes 835584 | tf_op jit(solution)/shard_map/all_gather | solution.py:71
  37.3 1.4 %copy.75 = bf16[512,768]{0,1:T(8,128)(2,1)S(1)} copy(bf16[512,768]{1,0:T(8,128)(2,1)} %all_gather.6) | data formatting | bytes 1572864 | tf_op jit(solution)/shard_map/all_gather | solution.py:71
  38.8 0.0 copy-done.9
  38.8 3.6 %convolution_convert_fusion.3 = bf16[512,768]{1,0:T(8,128)(2,1)S(1)} fusion(bf16[1536,768]{1,0:T(8,128)(2,1)} %param.10, bf16[512,1536]{1,0:T(8,128)(2,1)} %param.7, f32[1536]{0:T(1024)S(1)} %copy-done.9, f32[512]{0:T(512)S(1)} %add_rsqrt_fusion), kind=kOutput, calls=%fused_computation.21 | convolution fusion | flops 1211498496 | bytes 4726784 | tf_op jit(solution)/shard_map/dot_general | solution.py:45
  42.4 0.2 copy.70
  42.6 0.0 copy-start.4
  42.6 1.1 %fusion = (f32[2,4,6,64]{3,1,0,2:T(4,128)S(1)}, f32[6,512,2,4,64]{1,4,3,2,0:T(8,128)S(1)}) fusion(pred[2,512]{1,0:T(4,128)(4,1)S(1)} %broadcast_compare_fusion, bf16[512,6,128,1,1]{0,2,4,3,1:T(8,128)(2,1)S(1)} %bitcast.70, bf16[2,4,64,6,128]{4,2,1,0,3:T(8,128)(2,1)S(1)} %bitcast.68), kind=kOutput, calls=%fused_computation.2 | convolution fusion | flops 407368704 | bytes 7877632 | tf_op jit(solution)/shard_map/fnqhd,khd->fnhqk/dot_general | solution.py:82
  43.7 0.0 copy-done.4
  43.7 0.2 copy.71
  43.9 0.6 fusion.23
  44.5 0.0 copy-start.1
  44.6 0.0 copy-start.7
  44.6 0.0 copy-start.8
  44.6 3.1 %fusion.1 = (f32[2,4,6,64]{3,1,0,2:T(4,128)S(1)}, bf16[2,4,6,64,512]{4,3,1,0,2:T(8,128)(2,1)}) fusion(f32[6,512,2,4,64]{1,4,3,2,0:T(8,128)S(1)} %get-tuple-element.12, f32[2,4,6,64]{3,1,0,2:T(4,128)S(1)} %copy.80, pred[2,512]{1,0:T(4,128)(4,1)S(1)} %broadcast_compare_fusion), kind=kLoop, calls=%fused_computation.3 | loop fusion | flops 9434112 | bytes 9462784 | tf_op jit(solution)/shard_map/reduce_sum | solution.py:95
  47.7 0.0 copy-done.1
  47.7 0.4 fusion.10
  48.1 0.0 copy-done.7
  48.2 0.2 copy-done.8
  48.4 1.5 %convolution_convert_fusion.1 = bf16[512,768]{1,0:T(8,128)(2,1)S(1)} fusion(bf16[1536,768]{1,0:T(8,128)(2,1)S(1)} %copy-done.8, bf16[512,1536]{1,0:T(8,128)(2,1)S(1)} %copy-done.7, f32[1536]{0:T(1024)S(1)} %copy-done.9, f32[512]{0:T(512)S(1)} %add_rsqrt_fusion), kind=kOutput, calls=%fused_computation.19 | convolution fusion | flops 1211498496 | bytes 4726784 | tf_op jit(solution)/shard_map/dot_general | solution.py:47
  49.9 0.0 copy-start.5
  49.9 1.5 %reshape.125 = f32[2,4,4,4,4,768]{5,4,3,2,1,0:T(4,128)} reshape(bf16[512,768]{1,0:T(8,128)(2,1)S(1)} %convolution_convert_fusion.1) | data formatting | bytes 2359296 | tf_op jit(solution)/shard_map/convert_element_type | solution.py:34
  51.4 1.9 %reduce_sum.61 = f32[2,4,4,768]{3,2,1,0:T(4,128)S(1)} reduce(f32[2,4,4,4,4,768]{5,4,3,2,1,0:T(4,128)} %reshape.125, f32[]{:T(128)} %constant.15.clone.1), dimensions={2,4}, to_apply=%region_5.6 | reduce | flops 368640 | bytes 1671172 | tf_op jit(solution)/shard_map/reduce_sum | solution.py:37
  53.3 0.0 copy-done.5
  53.4 19.8 %all_gather.7 = bf16[512,768]{1,0:T(8,128)(2,1)S(1)} all-gather(bf16[32,768]{1,0:T(8,128)(2,1)S(1)} %convert_element_type.64), channel_id=1, replica_groups=mesh['grp'=2,'tm'=16] {'tm'}, dimensions={0}, use_global_device_ids=true | all-gather | bytes 835584 | tf_op jit(solution)/shard_map/all_gather | solution.py:72
  73.1 1.2 %copy.78 = bf16[512,768]{0,1:T(8,128)(2,1)} copy(bf16[512,768]{1,0:T(8,128)(2,1)S(1)} %all_gather.7) | data formatting | bytes 1572864 | tf_op jit(solution)/shard_map/all_gather | solution.py:72
  74.3 0.0 copy-start.6
  74.3 0.0 copy-start.2
  74.3 3.3 %fusion.6 = f32[6,128,2,4,64]{1,4,0,3,2:T(8,128)S(1)} fusion(bf16[512,6,128,1,1]{0,2,1,4,3:T(8,128)(2,1)} %bitcast.76, bf16[2,4,6,64,512]{4,3,1,0,2:T(8,128)(2,1)} %get-tuple-element.8), kind=kOutput, calls=%fused_computation.10 | convolution fusion | flops 402653184 | bytes 5505024 | tf_op jit(solution)/shard_map/fnhqk,khd->fnhqd/dot_general | solution.py:96
  77.6 0.0 copy-done.6
  77.6 0.2 copy.73
  77.8 0.0 copy-done.2
  77.8 1.5 %fusion.9 = bf16[2,4,64,6,128]{4,2,3,1,0:T(8,128)(2,1)S(1)} fusion(f32[6,128,2,4,64]{1,4,0,3,2:T(8,128)S(1)} %fusion.6, bf16[2,4,64,6,128]{4,2,3,1,0:T(8,128)(2,1)S(1)} %bitcast.75, f32[2,4,6,64,64]{3,4,2,1,0:T(8,128)S(1)} %copy-done.2, f32[2,4,64,6]{2,3,1,0:T(8,128)S(1)} %get-tuple-element.5, f32[2,4,64,6]{2,3,1,0:T(8,128)S(1)} %get-tuple-element.6, ...), kind=kOutput, calls=%fused_computation.15 | convolution fusion | flops 52297728 | bytes 3969024 | tf_op jit(solution)/shard_map/fnhqk,fnkhd->fnhqd/dot_general | solution.py:64
  79.3 0.6 copy.84
  79.8 1.8 %reshape.122 = bf16[2,2,2,8,8,768]{5,4,3,2,1,0:T(8,128)(2,1)} reshape(bf16[2,4,64,6,128]{4,3,2,1,0:T(8,128)(2,1)S(1)} %copy.84) | data formatting | bytes 1572864 | tf_op jit(solution)/shard_map/reshape | solution.py:27
  81.6 1.2 %copy.85 = bf16[2,2,8,2,8,768]{5,4,3,2,1,0:T(8,128)(2,1)S(1)} copy(bf16[2,2,8,2,8,768]{5,4,2,3,1,0:T(8,128)(2,1)} %bitcast.71) | data formatting | bytes 1572864 | tf_op jit(solution)/shard_map/transpose | solution.py:28
  82.8 0.0 copy-done
  82.8 2.5 %convolution_convert_fusion = bf16[512,1536]{1,0:T(8,128)(2,1)} fusion(bf16[512,768]{1,0:T(8,128)(2,1)S(1)} %bitcast.77, bf16[768,1536]{1,0:T(8,128)(2,1)S(1)} %copy-done), kind=kOutput, calls=%fused_computation.12 | convolution fusion | flops 1208745984 | bytes 4718592 | tf_op jit(solution)/shard_map/dot_general | solution.py:106
  (9 shorter events, 0.1 us)
Async XLA Ops:
  0.0 82.8 %copy-start = (bf16[768,1536]{1,0:T(8,128)(2,1)S(1)}, bf16[768,1536]{1,0:T(8,128)(2,1)}, u32[]{:S(2)}) copy-start(bf16[768,1536]{1,0:T(8,128)(2,1)} %param.13) | copy-start | bytes 7077892
  7.1 3.5 %copy-start.3 = (bf16[512,768]{1,0:T(8,128)(2,1)}, bf16[512,768]{1,0:T(8,128)(2,1)S(1)}, u32[]{:S(2)}) copy-start(bf16[512,768]{1,0:T(8,128)(2,1)S(1)} %convolution_convert_fusion.2) | copy-start | bytes 2359300
  8.6 30.1 %copy-start.9 = (f32[1536]{0:T(1024)S(1)}, f32[1536]{0:T(1024)}, u32[]{:S(2)}) copy-start(f32[1536]{0:T(1024)} %param.9) | copy-start | bytes 18436
  42.6 1.1 %copy-start.4 = (bf16[512,768]{1,0:T(8,128)(2,1)S(1)}, bf16[512,768]{1,0:T(8,128)(2,1)}, u32[]{:S(2)}) copy-start(bf16[512,768]{1,0:T(8,128)(2,1)} %copy-done.3) | copy-start | bytes 2359300
  44.5 3.2 %copy-start.1 = (f32[2,4,6,64,64]{3,4,2,1,0:T(8,128)}, f32[2,4,6,64,64]{3,4,2,1,0:T(8,128)S(1)}, u32[]{:S(2)}) copy-start(f32[2,4,6,64,64]{3,4,2,1,0:T(8,128)S(1)} %get-tuple-element.10) | copy-start | bytes 2359300
  44.6 3.6 %copy-start.7 = (bf16[512,1536]{1,0:T(8,128)(2,1)S(1)}, bf16[512,1536]{1,0:T(8,128)(2,1)}, u32[]{:S(2)}) copy-start(bf16[512,1536]{1,0:T(8,128)(2,1)} %param.7) | copy-start | bytes 4718596
  44.6 3.8 %copy-start.8 = (bf16[1536,768]{1,0:T(8,128)(2,1)S(1)}, bf16[1536,768]{1,0:T(8,128)(2,1)}, u32[]{:S(2)}) copy-start(bf16[1536,768]{1,0:T(8,128)(2,1)} %param.12) | copy-start | bytes 7077892
  49.9 3.5 %copy-start.5 = (bf16[512,768]{1,0:T(8,128)(2,1)}, bf16[512,768]{1,0:T(8,128)(2,1)S(1)}, u32[]{:S(2)}) copy-start(bf16[512,768]{1,0:T(8,128)(2,1)S(1)} %convolution_convert_fusion.1) | copy-start | bytes 2359300
  74.3 3.3 %copy-start.6 = (bf16[512,768]{1,0:T(8,128)(2,1)S(1)}, bf16[512,768]{1,0:T(8,128)(2,1)}, u32[]{:S(2)}) copy-start(bf16[512,768]{1,0:T(8,128)(2,1)} %copy-done.5) | copy-start | bytes 2359300
  74.3 3.5 %copy-start.2 = (f32[2,4,6,64,64]{3,4,2,1,0:T(8,128)S(1)}, f32[2,4,6,64,64]{3,4,2,1,0:T(8,128)}, u32[]{:S(2)}) copy-start(f32[2,4,6,64,64]{3,4,2,1,0:T(8,128)} %copy-done.1) | copy-start | bytes 2359300
where the time goes:
time: 85.7 us; the launch traced here: 85.4 us
  blocking collectives  46.5 us (54%)
  matrix products  17.6 us (21%)
  local copies, waits for them, and re-layouts  11 us (13%)
  other arithmetic  9.99 us (12%)
    all_gather x1, blocking collectives, on_device(): lax.all_gather(pooled_keys, 'tm', axis=0, tiled=True)  26.7 us
    all_gather x1, blocking collectives, on_device(): lax.all_gather(pooled_values, 'tm', axis=0, tiled=True)  19.8 us
    reduce_sum x2, other arithmetic, pooled(): jnp.mean(shaped, axis=(2, 4)).reshape(count * pool_rows, HEADS * HD)  3.78 us
    dot_general x1, matrix products, on_device(): jnp.dot(normed, w_key, preferred_element_type=jnp.float32)  3.6 us
    dot_general x1, matrix products, on_device(): jnp.dot(normed, w_query, preferred_element_type=jnp.float32)  3.58 us
    dot_general x1, matrix products, on_device(): jnp.einsum('fnhqk,khd->fnhqd', weights.astype(jnp.bfloat16), whole_values...  3.25 us
    reduce_sum x1, other arithmetic, on_device(): total = total * keep + jnp.sum(weights, -1)  3.13 us
    convert_element_type x2, local copies, waits for them, and re-layouts, pooled(): array.reshape(count, HH // POOL, POOL, WW // POOL, POOL, HEADS * HD)  3.03 us

commit v1 on v0

v1 whole, which is shorter than its diff:
```python
import functools

import jax
import jax.numpy as jnp
from jax import lax
from jax.experimental import pallas as pl
from jax.experimental.pallas import tpu as pltpu
from jax.sharding import PartitionSpec as P

HEADS = 6
HD = 128
HH = 16
WW = 16
WIN = 8
POOL = 4
TOKENS = HH * WW
PK = (HH // POOL) * (WW // POOL)
HALF = WIN * WW
NEG = -1e30
LOG2E = 1.4426950408889634
MESH = pl.DeviceIdType.MESH
NT = (((1,), (1,)), ((), ()))


def kernel(n, snake, ft, gain, x_hbm, wq_hbm, wk_hbm, wv_hbm, mixed,
           x_v, wq, wk, wv, normed, q_s, k_s, v_s, kg, vg, bias,
           x_sem, w_sem, ring_send, ring_recv, sib_send, sib_recv):
    rows = x_v.shape[0]
    count = rows // TOKENS
    own = count * PK
    keys = kg.shape[0]
    chips = n // 2
    me = lax.axis_index("tm")
    core = me % 2
    chip = me // 2
    half = chips // 2

    def chip_at(pos):
        pos = (pos + chips) % chips
        if not snake:
            return pos
        side = pos // half
        return (1 - side) * (2 * pos) + side * (2 * (chips - 1 - pos) + 1)

    if snake:
        place = (1 - chip % 2) * (chip // 2) + (chip % 2) * (chips - 1 - chip // 2)
    else:
        place = chip
    sibling = chip * 2 + (1 - core)
    step_of = (1, -1)
    neighbour = [chip_at(place + s) * 2 + core for s in step_of]
    reach = ((chips // 2, (chips - 1) // 2), ((chips - 1) // 2, chips // 2))

    blocks = x_sem.shape[0]
    size = rows // blocks
    loads = []
    for b in range(blocks):
        part = pl.ds(b * size, size)
        loads.append(pltpu.make_async_copy(x_hbm.at[part], x_v.at[part], x_sem.at[b]))
        loads[-1].start()
    weights = []
    for i, (src, dst) in enumerate(((wk_hbm, wk), (wv_hbm, wv), (wq_hbm, wq))):
        weights.append(pltpu.make_async_copy(src, dst, w_sem.at[i]))
        weights[-1].start()

    barrier = pltpu.get_barrier_semaphore()
    for other in (neighbour[0], neighbour[1], sibling):
        pl.semaphore_signal(barrier, inc=1, device_id={"tm": other}, device_id_type=MESH)

    slot = lax.broadcasted_iota(jnp.int32, (1, keys), 1) // PK

    def fill(s, kt):
        return jnp.where(slot == s, ft[s], kt)

    key_time = lax.fori_loop(0, ft.shape[0], fill, jnp.zeros((1, keys), jnp.int32))
    for f in range(count):
        bias[f] = jnp.where(key_time < ft[me * count + f], 0.0, NEG)

    sub = 32
    for b in range(blocks):
        loads[b].wait()

        def norm(i, carry, b=b):
            part = pl.ds(pl.multiple_of(b * size + i * sub, sub), sub)
            xf = x_v[part, :].astype(jnp.float32)
            scale = lax.rsqrt(jnp.mean(xf * xf, axis=-1, keepdims=True) + 1e-06)
            normed[part, :] = (xf * scale * gain[...]).astype(jnp.bfloat16)
            return carry

        lax.fori_loop(0, size // sub, norm, 0)

    tile = 256

    def project(w, out):
        def body(j, carry):
            cols = pl.ds(pl.multiple_of(j * tile, tile), tile)
            out[:, cols] = jnp.dot(
                normed[...], w[:, cols], preferred_element_type=jnp.float32
            ).astype(jnp.bfloat16)
            return carry

        lax.fori_loop(0, w.shape[1] // tile, body, 0)

    pr = lax.broadcasted_iota(jnp.int32, (own, rows), 0)
    pc = lax.broadcasted_iota(jnp.int32, (own, rows), 1)
    block_of = (pc // TOKENS) * PK + (pc % TOKENS) // (POOL * WW) * (WW // POOL) + (pc % WW) // POOL
    pool = jnp.where(pr == block_of, 1.0 / (POOL * POOL), 0.0).astype(jnp.bfloat16)

    gathered = (kg, vg)

    def rows_of(dev):
        return pl.ds(pl.multiple_of(dev * own, own), own)

    def origin(way, dist, plane):
        return chip_at(place - step_of[way] * dist) * 2 + plane

    def ring(way, dist, part):
        there = gathered[part].at[rows_of(origin(way, dist, core))]
        return pltpu.make_async_remote_copy(
            src_ref=there, dst_ref=there,
            send_sem=ring_send.at[way, dist, part], recv_sem=ring_recv.at[way, dist, part],
            device_id={"tm": neighbour[way]}, device_id_type=MESH)

    def arrived(way, dist, part):
        there = gathered[part].at[rows_of(origin(way, dist, core))]
        return pltpu.make_async_remote_copy(
            src_ref=there, dst_ref=there,
            send_sem=ring_send.at[way, dist - 1, part], recv_sem=ring_recv.at[way, dist - 1, part],
            device_id={"tm": neighbour[way]}, device_id_type=MESH)

    def across(way, dist, part, plane):
        there = gathered[part].at[rows_of(origin(way, dist, plane))]
        return pltpu.make_async_remote_copy(
            src_ref=there, dst_ref=there,
            send_sem=sib_send.at[way, dist, part], recv_sem=sib_recv.at[way, dist, part],
            device_id={"tm": sibling}, device_id_type=MESH)

    sends = []
    incoming = []

    def send_own(part):
        for way in (0, 1):
            if reach[way][part] > 0:
                copy = ring(way, 0, part)
                copy.start()
                sends.append(copy)
        copy = across(0, 0, part, core)
        copy.start()
        sends.append(copy)
        incoming.append(across(0, 0, part, 1 - core))

    def relay(dist, part):
        for way in (0, 1):
            if dist > reach[way][part]:
                continue
            arrived(way, dist, part).wait_recv()
            if dist < reach[way][part]:
                copy = ring(way, dist, part)
                copy.start()
                sends.append(copy)
            copy = across(way, dist, part, core)
            copy.start()
            sends.append(copy)
            incoming.append(across(way, dist, part, 1 - core))

    weights[0].wait()
    project(wk, k_s)
    kg[rows_of(me), :] = jnp.dot(pool, k_s[...], preferred_element_type=jnp.float32).astype(jnp.bfloat16)
    pl.semaphore_wait(barrier, 3)
    send_own(0)
    weights[1].wait()
    project(wv, v_s)
    vg[rows_of(me), :] = jnp.dot(pool, v_s[...], preferred_element_type=jnp.float32).astype(jnp.bfloat16)
    send_own(1)
    weights[2].wait()
    project(wq, q_s)
    for dist in range(1, chips // 2 + 1):
        for part in (0, 1):
            relay(dist, part)
    for copy in incoming:
        copy.wait_recv()

    ir = lax.broadcasted_iota(jnp.int32, (HALF, HALF), 0)
    ic = lax.broadcasted_iota(jnp.int32, (HALF, HALF), 1)
    near_bias = jnp.where((ir // WIN) % 2 == (ic // WIN) % 2, 0.0, NEG)
    rate = LOG2E / HD**0.5

    def attend(i, carry):
        f = i // (HEADS * 2)
        part = (i // HEADS) % 2
        h = i % HEADS
        cols = pl.ds(pl.multiple_of(h * HD, HD), HD)
        here = pl.ds(pl.multiple_of(f * TOKENS + part * HALF, HALF), HALF)
        q = q_s[here, cols]
        near = lax.dot_general(q, k_s[here, cols], NT, preferred_element_type=jnp.float32) + near_bias
        far = lax.dot_general(q, kg[:, cols], NT, preferred_element_type=jnp.float32) + bias[f]
        top = jnp.maximum(jnp.max(near, -1, keepdims=True), jnp.max(far, -1, keepdims=True))
        near_w = jnp.exp2((near - top) * rate)
        far_w = jnp.exp2((far - top) * rate)
        total = jnp.sum(near_w, -1, keepdims=True) + jnp.sum(far_w, -1, keepdims=True)
        acc = jnp.dot(near_w.astype(jnp.bfloat16), v_s[here, cols], preferred_element_type=jnp.float32)
        acc = acc + jnp.dot(far_w.astype(jnp.bfloat16), vg[:, cols], preferred_element_type=jnp.float32)
        mixed[here, cols] = (acc / total).astype(jnp.bfloat16)
        return carry

    lax.fori_loop(0, count * 2 * HEADS, attend, 0)
    for copy in sends:
        copy.wait_send()


def on_device(n, snake, frames_in, frame_time, norm_gain, w_query, w_key, w_value, w_output):
    rows, width = frames_in.shape
    inner = w_query.shape[1]
    count = rows // TOKENS
    keys = n * count * PK
    hops = n // 4 + 1
    bf = jnp.bfloat16
    dma = pltpu.SemaphoreType.DMA
    hbm = pl.BlockSpec(memory_space=pl.ANY)
    vmem = pl.BlockSpec(memory_space=pltpu.VMEM)
    mixed = pl.pallas_call(
        functools.partial(kernel, n, snake),
        out_shape=jax.ShapeDtypeStruct((rows, inner), bf),
        in_specs=[pl.BlockSpec(memory_space=pltpu.SMEM), vmem, hbm, hbm, hbm, hbm],
        out_specs=vmem,
        scratch_shapes=[
            pltpu.VMEM((rows, width), bf),
            pltpu.VMEM((width, inner), bf),
            pltpu.VMEM((width, inner), bf),
            pltpu.VMEM((width, inner), bf),
            pltpu.VMEM((rows, width), bf),
            pltpu.VMEM((rows, inner), bf),
            pltpu.VMEM((rows, inner), bf),
            pltpu.VMEM((rows, inner), bf),
            pltpu.VMEM((keys, inner), bf),
            pltpu.VMEM((keys, inner), bf),
            pltpu.VMEM((count, 1, keys), jnp.float32),
            dma((4,)),
            dma((3,)),
            dma((2, hops, 2)),
            dma((2, hops, 2)),
            dma((2, hops, 2)),
            dma((2, hops, 2)),
        ],
        compiler_params=pltpu.CompilerParams(
            collective_id=0, has_side_effects=True, vmem_limit_bytes=56 << 20
        ),
    )(frame_time, norm_gain.reshape(1, width), frames_in, w_query, w_key, w_value)
    return jnp.dot(mixed, w_output, preferred_element_type=jnp.float32).astype(bf)


def is_snake(mesh):
    names = list(mesh.axis_names)
    line = mesh.devices.transpose(names.index("grp"), names.index("tm"))[0]
    try:
        second = {d.coords[1] for d in line}
        third = {d.coords[2] for d in line}
    except (AttributeError, TypeError):
        return False
    return len(second) == 2 and len(third) * 4 == len(line)


def solution(mesh):
    placed = (P(("grp", "tm"), None), P("grp"), P(), P(), P(), P(), P())
    n = mesh.shape["tm"]
    return jax.shard_map(
        functools.partial(on_device, n, is_snake(mesh)),
        mesh=mesh, in_specs=placed, out_specs=P(("grp", "tm"), None), check_vma=False,
    )
```

time: 85.7 us -> 44.1 us (0.51)
  the two profiles are of different devices: /device:TPU:0 before, /device:TPU:1 now
where the time goes in v1:
time: 44.1 us; the launch traced here: 43.8 us
  Pallas kernels  38.7 us (88%)
  matrix products  3.66 us (8%)
  local copies, waits for them, and re-layouts  1.45 us (3%)
    pallas_call x1, Pallas kernels, on_device(): pl.pallas_call(functools.partial(kernel, n, snake), out_shape=jax.ShapeDt...  38.7 us
    dot_general x1, matrix products, on_device(): jnp.dot(mixed, w_output, preferred_element_type=jnp.float32).astype(bf)  3.66 us
    reshape x1, local copies, waits for them, and re-layouts, on_device(): norm_gain.reshape(1, width)  1.44 us

profile of v1, /device:TPU:1, one launch (start us, length us, event | category | flops | bytes accessed | tf_op | source)
XLA Modules:
  0.0 43.8 jit_solution(7645690133858027037)
XLA Ops:
  0.0 0.0 copy-start
  0.0 1.4 %reshape.3.gain = f32[1,1536]{1,0:T(1,128)} reshape(f32[1536]{0:T(1024)} %param.9) | data formatting | bytes 12288 | tf_op jit(solution)/shard_map/reshape | solution.py:248
  1.4 38.7 %shard_map.73 = bf16[512,768]{1,0:T(8,128)(2,1)} custom-call(s32[32]{0:T(128)} %ft.1, f32[1,1536]{1,0:T(1,128)} %reshape.3.gain, bf16[512,1536]{1,0:T(8,128)(2,1)} %x_hbm.1, bf16[1536,768]{1,0:T(8,128)(2,1)} %wq_hbm.1, bf16[1536,768]{1,0:T(8,128)(2,1)} %wk_hbm.1, bf16[1536,768]{1,0:T(8,128)(2,1)} %wv_hbm.1), custom_call_target="tpu_custom_call" | custom-call | tf_op jit(solution)/shard_map/pallas_call | solution.py:221
  40.2 0.0 copy-done
  40.2 3.7 %convolution_convert_fusion = bf16[512,1536]{1,0:T(8,128)(2,1)} fusion(bf16[512,768]{1,0:T(8,128)(2,1)} %shard_map.73, bf16[768,1536]{1,0:T(8,128)(2,1)S(1)} %copy-done), kind=kOutput, calls=%fused_computation | convolution fusion | flops 1208745984 | bytes 4718592 | tf_op jit(solution)/shard_map/dot_general | solution.py:249
Async XLA Ops:
  0.0 40.2 %copy-start = (bf16[768,1536]{1,0:T(8,128)(2,1)S(1)}, bf16[768,1536]{1,0:T(8,128)(2,1)}, u32[]{:S(2)}) copy-start(bf16[768,1536]{1,0:T(8,128)(2,1)} %param.13) | copy-start | bytes 7077892

commit v2 on v1

v2 whole, which is shorter than its diff:
```python
import functools

import jax
import jax.numpy as jnp
from jax import lax
from jax.experimental import pallas as pl
from jax.experimental.pallas import tpu as pltpu
from jax.sharding import PartitionSpec as P

HEADS = 6
HD = 128
HH = 16
WW = 16
WIN = 8
POOL = 4
TOKENS = HH * WW
PK = (HH // POOL) * (WW // POOL)
HALF = WIN * WW
NEG = -1e30
LOG2E = 1.4426950408889634
MESH = pl.DeviceIdType.MESH
NT = (((1,), (1,)), ((), ()))


def kernel(n, snake, near_reach, ft, gain, x_hbm, wq_hbm, wk_hbm, wv_hbm, mixed,
           x_v, wq, wk, wv, normed, q_s, k_s, v_s, far, bias, top_s, total_s, acc_s,
           x_sem, w_sem, ring_send, ring_recv, sib_send, sib_recv):
    rows = x_v.shape[0]
    count = rows // TOKENS
    own = count * PK
    pieces, keys, tile = far.shape
    parts = pieces // 2
    chips = n // 2
    me = lax.axis_index("tm")
    core = me % 2
    chip = me // 2
    half = chips // 2
    reach = (chips // 2, (chips - 1) // 2)

    def chip_at(pos):
        pos = (pos + chips) % chips
        if not snake:
            return pos
        side = pos // half
        return (1 - side) * (2 * pos) + side * (2 * (chips - 1 - pos) + 1)

    if snake:
        place = (1 - chip % 2) * (chip // 2) + (chip % 2) * (chips - 1 - chip // 2)
    else:
        place = chip
    sibling = chip * 2 + (1 - core)
    step_of = (1, -1)
    neighbour = [chip_at(place + s) * 2 + core for s in step_of]

    def limit(way, piece):
        return reach[way] if piece < parts else reach[1 - way]

    def place_of(way, dist, cross):
        if dist == 0:
            return cross * own
        first = (4 * dist - 2) * own
        if 2 * dist == chips:
            return first + cross * own
        return first + (2 * way + cross) * own

    blocks = x_sem.shape[0]
    size = rows // blocks
    loads = []
    for b in range(blocks):
        part = pl.ds(b * size, size)
        loads.append(pltpu.make_async_copy(x_hbm.at[part], x_v.at[part], x_sem.at[b]))
        loads[-1].start()
    weights = []
    for i, (src, dst) in enumerate(((wk_hbm, wk), (wv_hbm, wv), (wq_hbm, wq))):
        weights.append(pltpu.make_async_copy(src, dst, w_sem.at[i]))
        weights[-1].start()

    barrier = pltpu.get_barrier_semaphore()
    for other in (neighbour[0], neighbour[1], sibling):
        pl.semaphore_signal(barrier, inc=1, device_id={"tm": other}, device_id_type=MESH)

    sub = 32
    for b in range(blocks):
        loads[b].wait()

        def norm(i, carry, b=b):
            part = pl.ds(pl.multiple_of(b * size + i * sub, sub), sub)
            xf = x_v[part, :].astype(jnp.float32)
            scale = lax.rsqrt(jnp.mean(xf * xf, axis=-1, keepdims=True) + 1e-06)
            normed[part, :] = (xf * scale * gain[...]).astype(jnp.bfloat16)
            return carry

        lax.fori_loop(0, size // sub, norm, 0)

    pr = lax.broadcasted_iota(jnp.int32, (own, rows), 0)
    pc = lax.broadcasted_iota(jnp.int32, (own, rows), 1)
    block_of = (pc // TOKENS) * PK + (pc % TOKENS) // (POOL * WW) * (WW // POOL) + (pc % WW) // POOL
    pool = jnp.where(pr == block_of, 1.0 / (POOL * POOL), 0.0).astype(jnp.bfloat16)

    def ring(way, dist, piece):
        return pltpu.make_async_remote_copy(
            src_ref=far.at[piece, pl.ds(place_of(way, dist, 0), own)],
            dst_ref=far.at[piece, pl.ds(place_of(way, dist + 1, 0), own)],
            send_sem=ring_send.at[way, dist, piece], recv_sem=ring_recv.at[way, dist, piece],
            device_id={"tm": neighbour[way]}, device_id_type=MESH)

    def across(way, dist, piece):
        return pltpu.make_async_remote_copy(
            src_ref=far.at[piece, pl.ds(place_of(way, dist, 0), own)],
            dst_ref=far.at[piece, pl.ds(place_of(way, dist, 1), own)],
            send_sem=sib_send.at[way, dist, piece], recv_sem=sib_recv.at[way, dist, piece],
            device_id={"tm": sibling}, device_id_type=MESH)

    sends = []
    incoming = {}

    def send(way, dist, piece):
        if dist < limit(way, piece):
            copy = ring(way, dist, piece)
            copy.start()
            sends.append(copy)

    def share(way, dist, piece):
        copy = across(way, dist, piece)
        copy.start()
        sends.append(copy)
        incoming.setdefault(dist, []).append(copy)

    def relay(dist):
        for piece in range(pieces):
            for way in (0, 1):
                if dist <= limit(way, piece):
                    ring(way, dist - 1, piece).wait_recv()
                    send(way, dist, piece)
                    share(way, dist, piece)

    def settle(dists):
        for dist in dists:
            for copy in incoming[dist]:
                copy.wait_recv()

    def project(w, out, j):
        cols = pl.ds(j * tile, tile)
        out[:, cols] = jnp.dot(
            normed[...], w[:, cols], preferred_element_type=jnp.float32
        ).astype(jnp.bfloat16)

    for base, weight, w, out in ((0, weights[0], wk, k_s), (parts, weights[1], wv, v_s)):
        weight.wait()
        for j in range(parts):
            project(w, out, j)
            far[base + j, pl.ds(0, own), :] = jnp.dot(
                pool, out[:, pl.ds(j * tile, tile)], preferred_element_type=jnp.float32
            ).astype(jnp.bfloat16)
            if base + j == 0:
                pl.semaphore_wait(barrier, 3)
            for way in (0, 1):
                send(way, 0, base + j)
            share(0, 0, base + j)

    slot = lax.broadcasted_iota(jnp.int32, (1, keys), 1) // PK
    key_time = jnp.zeros((1, keys), jnp.int32)
    for dist in range(reach[0] + 1):
        for way in (0, 1):
            if (dist == 0 or 2 * dist == chips) and way == 1:
                continue
            for cross in (0, 1):
                plane = core * (1 - cross) + (1 - core) * cross
                dev = chip_at(place - step_of[way] * dist) * 2 + plane
                first = place_of(way, dist, cross) // PK
                for f in range(count):
                    key_time = jnp.where(slot == first + f, ft[dev * count + f], key_time)
    for f in range(count):
        bias[f] = jnp.where(key_time < ft[me * count + f], 0.0, NEG)

    weights[2].wait()
    for j in range(parts):
        project(wq, q_s, j)

    ir = lax.broadcasted_iota(jnp.int32, (HALF, HALF), 0)
    ic = lax.broadcasted_iota(jnp.int32, (HALF, HALF), 1)
    near_bias = jnp.where((ir // WIN) % 2 == (ic // WIN) % 2, 0.0, NEG)
    rate = LOG2E / HD**0.5
    cut = min(keys, (4 * near_reach + 2) * own)
    groups = tile // HD

    def first_pass(h, carry):
        cols = pl.ds(pl.multiple_of(h * HD, HD), HD)
        inner = pl.ds(pl.multiple_of(h % groups * HD, HD), HD)
        k_far = far[h // groups, pl.ds(0, cut), inner]
        v_far = far[parts + h // groups, pl.ds(0, cut), inner]
        for block in range(rows // HALF):
            here = pl.ds(block * HALF, HALF)
            q = q_s[here, cols]
            s0 = lax.dot_general(q, k_s[here, cols], NT, preferred_element_type=jnp.float32) + near_bias
            s1 = lax.dot_general(q, k_far, NT, preferred_element_type=jnp.float32)
            s1 = s1 + bias[block * HALF // TOKENS, :, pl.ds(0, cut)]
            top = jnp.maximum(jnp.max(s0, -1, keepdims=True), jnp.max(s1, -1, keepdims=True))
            w0 = jnp.exp2((s0 - top) * rate)
            w1 = jnp.exp2((s1 - top) * rate)
            total_s[h, here, :] = jnp.sum(w0, -1, keepdims=True) + jnp.sum(w1, -1, keepdims=True)
            top_s[h, here, :] = top
            acc = jnp.dot(w0.astype(jnp.bfloat16), v_s[here, cols], preferred_element_type=jnp.float32)
            acc_s[h, here, :] = acc + jnp.dot(w1.astype(jnp.bfloat16), v_far, preferred_element_type=jnp.float32)
        return carry

    def second_pass(h, carry):
        cols = pl.ds(pl.multiple_of(h * HD, HD), HD)
        inner = pl.ds(pl.multiple_of(h % groups * HD, HD), HD)
        k_far = far[h // groups, pl.ds(cut, keys - cut), inner]
        v_far = far[parts + h // groups, pl.ds(cut, keys - cut), inner]
        for block in range(rows // HALF):
            here = pl.ds(block * HALF, HALF)
            q = q_s[here, cols]
            s1 = lax.dot_general(q, k_far, NT, preferred_element_type=jnp.float32)
            s1 = s1 + bias[block * HALF // TOKENS, :, pl.ds(cut, keys - cut)]
            old = top_s[h, here, :]
            top = jnp.maximum(old, jnp.max(s1, -1, keepdims=True))
            keep = jnp.exp2((old - top) * rate)
            w1 = jnp.exp2((s1 - top) * rate)
            total = total_s[h, here, :] * keep + jnp.sum(w1, -1, keepdims=True)
            acc = jnp.dot(w1.astype(jnp.bfloat16), v_far, preferred_element_type=jnp.float32)
            acc = acc_s[h, here, :] * keep + acc
            mixed[here, cols] = (acc / total).astype(jnp.bfloat16)
        return carry

    for dist in range(1, near_reach + 1):
        relay(dist)
    settle(range(near_reach + 1))
    later = list(range(near_reach + 1, reach[0] + 1))
    spread = HEADS // 2
    lax.fori_loop(0, spread, first_pass, 0)
    for dist in later[:1]:
        relay(dist)
    lax.fori_loop(spread, HEADS, first_pass, 0)
    for dist in later[1:]:
        relay(dist)
    settle(later)
    lax.fori_loop(0, HEADS, second_pass, 0)
    for copy in sends:
        copy.wait_send()


def on_device(n, snake, frames_in, frame_time, norm_gain, w_query, w_key, w_value, w_output):
    rows, width = frames_in.shape
    inner = w_query.shape[1]
    count = rows // TOKENS
    keys = n * count * PK
    hops = n // 4 + 1
    tile = 2 * HD
    pieces = 2 * (inner // tile)
    near_reach = n // 8
    bf = jnp.bfloat16
    f32 = jnp.float32
    dma = pltpu.SemaphoreType.DMA
    hbm = pl.BlockSpec(memory_space=pl.ANY)
    vmem = pl.BlockSpec(memory_space=pltpu.VMEM)
    mixed = pl.pallas_call(
        functools.partial(kernel, n, snake, near_reach),
        out_shape=jax.ShapeDtypeStruct((rows, inner), bf),
        in_specs=[pl.BlockSpec(memory_space=pltpu.SMEM), vmem, hbm, hbm, hbm, hbm],
        out_specs=vmem,
        scratch_shapes=[
            pltpu.VMEM((rows, width), bf),
            pltpu.VMEM((width, inner), bf),
            pltpu.VMEM((width, inner), bf),
            pltpu.VMEM((width, inner), bf),
            pltpu.VMEM((rows, width), bf),
            pltpu.VMEM((rows, inner), bf),
            pltpu.VMEM((rows, inner), bf),
            pltpu.VMEM((rows, inner), bf),
            pltpu.VMEM((pieces, keys, tile), bf),
            pltpu.VMEM((count, 1, keys), f32),
            pltpu.VMEM((HEADS, rows, 1), f32),
            pltpu.VMEM((HEADS, rows, 1), f32),
            pltpu.VMEM((HEADS, rows, HD), f32),
            dma((4,)),
            dma((3,)),
            dma((2, hops, pieces)),
            dma((2, hops, pieces)),
            dma((2, hops, pieces)),
            dma((2, hops, pieces)),
        ],
        compiler_params=pltpu.CompilerParams(
            collective_id=0, has_side_effects=True, vmem_limit_bytes=56 << 20
        ),
    )(frame_time, norm_gain, frames_in, w_query, w_key, w_value)
    return jnp.dot(mixed, w_output, preferred_element_type=f32).astype(bf)


def is_snake(mesh):
    names = list(mesh.axis_names)
    line = mesh.devices.transpose(names.index("grp"), names.index("tm"))[0]
    try:
        second = {d.coords[1] for d in line}
        third = {d.coords[2] for d in line}
    except (AttributeError, TypeError):
        return False
    return len(second) == 2 and len(third) * 4 == len(line)


def solution(mesh):
    placed = (P(("grp", "tm"), None), P("grp"), P(), P(), P(), P(), P())
    n = mesh.shape["tm"]
    return jax.shard_map(
        functools.partial(on_device, n, is_snake(mesh)),
        mesh=mesh, in_specs=placed, out_specs=P(("grp", "tm"), None), check_vma=False,
    )
```

time: 44.1 us -> 43.5 us (0.986)
  the two profiles are of different devices: /device:TPU:1 before, /device:TPU:0 now
where the time goes in v2:
time: 43.5 us; the launch traced here: 43.3 us
  Pallas kernels  39.6 us (91%)
  matrix products  3.66 us (8%)
    pallas_call x1, Pallas kernels, on_device(): pl.pallas_call(functools.partial(kernel, n, snake, near_reach), out_shape...  39.6 us
    dot_general x1, matrix products, on_device(): return jnp.dot(mixed, w_output, preferred_element_type=f32).astype(bf)  3.66 us

profile of v2, /device:TPU:0, one launch (start us, length us, event | category | flops | bytes accessed | tf_op | source)
XLA Modules:
  0.0 43.3 jit_solution(16018747198222308621)
XLA Ops:
  0.0 0.0 copy-start
  0.0 39.6 %shard_map.73 = bf16[512,768]{1,0:T(8,128)(2,1)} custom-call(s32[32]{0:T(128)} %ft.1, f32[1536]{0:T(1024)} %gain.1, bf16[512,1536]{1,0:T(8,128)(2,1)} %x_hbm.1, bf16[1536,768]{1,0:T(8,128)(2,1)} %wq_hbm.1, bf16[1536,768]{1,0:T(8,128)(2,1)} %wk_hbm.1, bf16[1536,768]{1,0:T(8,128)(2,1)} %wv_hbm.1), custom_call_target="tpu_custom_call" | custom-call | tf_op jit(solution)/shard_map/pallas_call | solution.py:258
  39.6 0.0 copy-done
  39.6 3.7 %convolution_convert_fusion = bf16[512,1536]{1,0:T(8,128)(2,1)} fusion(bf16[512,768]{1,0:T(8,128)(2,1)} %shard_map.73, bf16[768,1536]{1,0:T(8,128)(2,1)S(1)} %copy-done), kind=kOutput, calls=%fused_computation | convolution fusion | flops 1208745984 | bytes 4718592 | tf_op jit(solution)/shard_map/dot_general | solution.py:288
Async XLA Ops:
  0.0 39.6 %copy-start = (bf16[768,1536]{1,0:T(8,128)(2,1)S(1)}, bf16[768,1536]{1,0:T(8,128)(2,1)}, u32[]{:S(2)}) copy-start(bf16[768,1536]{1,0:T(8,128)(2,1)} %param.13) | copy-start | bytes 7077892

commit v3 on v2

--- a/solution.py
+++ b/solution.py
@@ -23,7 +23,7 @@
 
 
 def kernel(n, snake, near_reach, ft, gain, x_hbm, wq_hbm, wk_hbm, wv_hbm, mixed,
-           x_v, wq, wk, wv, normed, q_s, k_s, v_s, far, bias, top_s, total_s, acc_s,
+           x_v, wq, wk, wv, normed, q_s, k_s, v_s, far, bias, top_s, acc_s, s_s, p_s,
            x_sem, w_sem, ring_send, ring_recv, sib_send, sib_recv):
     rows = x_v.shape[0]
     count = rows // TOKENS
@@ -136,7 +136,7 @@
 
     def settle(dists):
         for dist in dists:
-            for copy in incoming[dist]:
+            for copy in incoming.get(dist, ()):
                 copy.wait_recv()
 
     def project(w, out, j):
@@ -184,44 +184,57 @@
     cut = min(keys, (4 * near_reach + 2) * own)
     groups = tile // HD
 
-    def first_pass(h, carry):
+    ones = jnp.ones((1, HD), jnp.bfloat16)
+
+    def with_ones(v):
+        return jnp.concatenate([v, jnp.broadcast_to(ones, v.shape)], axis=1)
+
+    def attend(h, lo, size, first, last):
         cols = pl.ds(pl.multiple_of(h * HD, HD), HD)
         inner = pl.ds(pl.multiple_of(h % groups * HD, HD), HD)
-        k_far = far[h // groups, pl.ds(0, cut), inner]
-        v_far = far[parts + h // groups, pl.ds(0, cut), inner]
+        span = pl.ds(0, size)
+        k_far = far[h // groups, pl.ds(lo, size), inner]
+        v_far = far[parts + h // groups, pl.ds(lo, size), inner]
+        s_s[:, span] = lax.dot_general(q_s[:, cols], k_far, NT, preferred_element_type=jnp.float32)
+        near = []
+        keeps = []
         for block in range(rows // HALF):
             here = pl.ds(block * HALF, HALF)
-            q = q_s[here, cols]
-            s0 = lax.dot_general(q, k_s[here, cols], NT, preferred_element_type=jnp.float32) + near_bias
-            s1 = lax.dot_general(q, k_far, NT, preferred_element_type=jnp.float32)
-            s1 = s1 + bias[block * HALF // TOKENS, :, pl.ds(0, cut)]
-            top = jnp.maximum(jnp.max(s0, -1, keepdims=True), jnp.max(s1, -1, keepdims=True))
-            w0 = jnp.exp2((s0 - top) * rate)
-            w1 = jnp.exp2((s1 - top) * rate)
-            total_s[h, here, :] = jnp.sum(w0, -1, keepdims=True) + jnp.sum(w1, -1, keepdims=True)
-            top_s[h, here, :] = top
-            acc = jnp.dot(w0.astype(jnp.bfloat16), v_s[here, cols], preferred_element_type=jnp.float32)
-            acc_s[h, here, :] = acc + jnp.dot(w1.astype(jnp.bfloat16), v_far, preferred_element_type=jnp.float32)
-        return carry
-
-    def second_pass(h, carry):
-        cols = pl.ds(pl.multiple_of(h * HD, HD), HD)
-        inner = pl.ds(pl.multiple_of(h % groups * HD, HD), HD)
-        k_far = far[h // groups, pl.ds(cut, keys - cut), inner]
-        v_far = far[parts + h // groups, pl.ds(cut, keys - cut), inner]
+            s = s_s[here, span] + bias[block * HALF // TOKENS, :, pl.ds(lo, size)]
+            if first:
+                s0 = lax.dot_general(q_s[here, cols], k_s[here, cols], NT, preferred_element_type=jnp.float32)
+                s = jnp.concatenate([s0 + near_bias, s], axis=1)
+            top = jnp.broadcast_to(jnp.max(s, -1, keepdims=True), (HALF, HD))
+            if not first:
+                old = top_s[h, here, :]
+                top = jnp.maximum(old, top)
+                keeps.append(jnp.exp2((old - top) * rate))
+            if not last:
+                top_s[h, here, :] = top
+            w = jnp.exp2((s - jnp.tile(top, (1, -(-s.shape[1] // HD)))[:, :s.shape[1]]) * rate).astype(jnp.bfloat16)
+            if first:
+                near.append(jnp.dot(w[:, :HD], with_ones(v_s[here, cols]), preferred_element_type=jnp.float32))
+                w = w[:, HD:]
+            p_s[here, span] = w
+        acc = jnp.dot(p_s[:, span], with_ones(v_far), preferred_element_type=jnp.float32)
         for block in range(rows // HALF):
             here = pl.ds(block * HALF, HALF)
-            q = q_s[here, cols]
-            s1 = lax.dot_general(q, k_far, NT, preferred_element_type=jnp.float32)
-            s1 = s1 + bias[block * HALF // TOKENS, :, pl.ds(cut, keys - cut)]
-            old = top_s[h, here, :]
-            top = jnp.maximum(old, jnp.max(s1, -1, keepdims=True))
-            keep = jnp.exp2((old - top) * rate)
-            w1 = jnp.exp2((s1 - top) * rate)
-            total = total_s[h, here, :] * keep + jnp.sum(w1, -1, keepdims=True)
-            acc = jnp.dot(w1.astype(jnp.bfloat16), v_far, preferred_element_type=jnp.float32)
-            acc = acc_s[h, here, :] * keep + acc
-            mixed[here, cols] = (acc / total).astype(jnp.bfloat16)
+            mine = acc[block * HALF:(block + 1) * HALF]
+            if first:
+                mine = mine + near[block]
+            else:
+                mine = mine + acc_s[h, here, :] * jnp.tile(keeps[block], (1, 2))
+            if last:
+                mixed[here, cols] = (mine[:, :HD] / mine[:, HD:]).astype(jnp.bfloat16)
+            else:
+                acc_s[h, here, :] = mine
+
+    def first_pass(h, carry):
+        attend(h, 0, cut, True, cut == keys)
+        return carry
+
+    def second_pass(h, carry):
+        attend(h, cut, keys - cut, False, True)
         return carry
 
     for dist in range(1, near_reach + 1):
@@ -236,7 +249,8 @@
     for dist in later[1:]:
         relay(dist)
     settle(later)
-    lax.fori_loop(0, HEADS, second_pass, 0)
+    if cut < keys:
+        lax.fori_loop(0, HEADS, second_pass, 0)
     for copy in sends:
         copy.wait_send()
 
@@ -271,9 +285,10 @@
             pltpu.VMEM((rows, inner), bf),
             pltpu.VMEM((pieces, keys, tile), bf),
             pltpu.VMEM((count, 1, keys), f32),
-            pltpu.VMEM((HEADS, rows, 1), f32),
-            pltpu.VMEM((HEADS, rows, 1), f32),
             pltpu.VMEM((HEADS, rows, HD), f32),
+            pltpu.VMEM((HEADS, rows, 2 * HD), f32),
+            pltpu.VMEM((rows, keys), f32),
+            pltpu.VMEM((rows, keys), bf),
             dma((4,)),
             dma((3,)),
             dma((2, hops, pieces)),

time: 43.5 us -> 37.8 us (0.87)
  Pallas kernels: 39.6 us -> 34 us
    pallas_call x1, Pallas kernels: 39.6 us -> 34 us  [on_device(): pl.pallas_call(functools.partial(kernel, n, snake, near_reach), out_shape...]
where the time goes in v3:
time: 37.8 us; the launch traced here: 37.6 us
  Pallas kernels  34 us (90%)
  matrix products  3.66 us (10%)
    pallas_call x1, Pallas kernels, on_device(): pl.pallas_call(functools.partial(kernel, n, snake, near_reach), out_shape...  34 us
    dot_general x1, matrix products, on_device(): return jnp.dot(mixed, w_output, preferred_element_type=f32).astype(bf)  3.66 us

profile of v3, /device:TPU:0, one launch (start us, length us, event | category | flops | bytes accessed | tf_op | source)
XLA Modules:
  0.0 37.6 jit_solution(4066472226795666036)
XLA Ops:
  0.0 0.0 copy-start
  0.0 34.0 %shard_map.73 = bf16[512,768]{1,0:T(8,128)(2,1)} custom-call(s32[32]{0:T(128)} %ft.1, f32[1536]{0:T(1024)} %gain.1, bf16[512,1536]{1,0:T(8,128)(2,1)} %x_hbm.1, bf16[1536,768]{1,0:T(8,128)(2,1)} %wq_hbm.1, bf16[1536,768]{1,0:T(8,128)(2,1)} %wk_hbm.1, bf16[1536,768]{1,0:T(8,128)(2,1)} %wv_hbm.1), custom_call_target="tpu_custom_call" | custom-call | tf_op jit(solution)/shard_map/pallas_call | solution.py:272
  34.0 0.0 copy-done
  34.0 3.7 %convolution_convert_fusion = bf16[512,1536]{1,0:T(8,128)(2,1)} fusion(bf16[512,768]{1,0:T(8,128)(2,1)} %shard_map.73, bf16[768,1536]{1,0:T(8,128)(2,1)S(1)} %copy-done), kind=kOutput, calls=%fused_computation | convolution fusion | flops 1208745984 | bytes 4718592 | tf_op jit(solution)/shard_map/dot_general | solution.py:303
Async XLA Ops:
  0.0 34.0 %copy-start = (bf16[768,1536]{1,0:T(8,128)(2,1)S(1)}, bf16[768,1536]{1,0:T(8,128)(2,1)}, u32[]{:S(2)}) copy-start(bf16[768,1536]{1,0:T(8,128)(2,1)} %param.13) | copy-start | bytes 7077892

commit v4 on v3

--- a/solution.py
+++ b/solution.py
@@ -50,7 +50,7 @@
         place = chip
     sibling = chip * 2 + (1 - core)
     step_of = (1, -1)
-    neighbour = [chip_at(place + s) * 2 + core for s in step_of]
+    neighbour = [[chip_at(place + s * jump) * 2 + core for jump in (1, 2)] for s in step_of]
 
     def limit(way, piece):
         return reach[way] if piece < parts else reach[1 - way]
@@ -76,7 +76,7 @@
         weights[-1].start()
 
     barrier = pltpu.get_barrier_semaphore()
-    for other in (neighbour[0], neighbour[1], sibling):
+    for other in (*neighbour[0], *neighbour[1], sibling):
         pl.semaphore_signal(barrier, inc=1, device_id={"tm": other}, device_id_type=MESH)
 
     sub = 32
@@ -97,12 +97,12 @@
     block_of = (pc // TOKENS) * PK + (pc % TOKENS) // (POOL * WW) * (WW // POOL) + (pc % WW) // POOL
     pool = jnp.where(pr == block_of, 1.0 / (POOL * POOL), 0.0).astype(jnp.bfloat16)
 
-    def ring(way, dist, piece):
+    def ring(way, dist, to, piece):
         return pltpu.make_async_remote_copy(
             src_ref=far.at[piece, pl.ds(place_of(way, dist, 0), own)],
-            dst_ref=far.at[piece, pl.ds(place_of(way, dist + 1, 0), own)],
-            send_sem=ring_send.at[way, dist, piece], recv_sem=ring_recv.at[way, dist, piece],
-            device_id={"tm": neighbour[way]}, device_id_type=MESH)
+            dst_ref=far.at[piece, pl.ds(place_of(way, to, 0), own)],
+            send_sem=ring_send.at[way, to - 1, piece], recv_sem=ring_recv.at[way, to - 1, piece],
+            device_id={"tm": neighbour[way][to - dist - 1]}, device_id_type=MESH)
 
     def across(way, dist, piece):
         return pltpu.make_async_remote_copy(
@@ -115,10 +115,11 @@
     incoming = {}
 
     def send(way, dist, piece):
-        if dist < limit(way, piece):
-            copy = ring(way, dist, piece)
-            copy.start()
-            sends.append(copy)
+        for to in (dist + 2, dist + 1):
+            if dist % 2 == 0 and to <= limit(way, piece):
+                copy = ring(way, dist, to, piece)
+                copy.start()
+                sends.append(copy)
 
     def share(way, dist, piece):
         copy = across(way, dist, piece)
@@ -130,7 +131,7 @@
         for piece in range(pieces):
             for way in (0, 1):
                 if dist <= limit(way, piece):
-                    ring(way, dist - 1, piece).wait_recv()
+                    ring(way, (dist - 1) // 2 * 2, dist, piece).wait_recv()
                     send(way, dist, piece)
                     share(way, dist, piece)
 
@@ -153,7 +154,7 @@
                 pool, out[:, pl.ds(j * tile, tile)], preferred_element_type=jnp.float32
             ).astype(jnp.bfloat16)
             if base + j == 0:
-                pl.semaphore_wait(barrier, 3)
+                pl.semaphore_wait(barrier, 5)
             for way in (0, 1):
                 send(way, 0, base + j)
             share(0, 0, base + j)

time: 37.8 us -> 36.3 us (0.960)
  the two profiles are of different devices: /device:TPU:0 before, /device:TPU:1 now
where the time goes in v4:
time: 36.3 us; the launch traced here: 36.1 us
  Pallas kernels  32.4 us (89%)
  matrix products  3.67 us (10%)
    pallas_call x1, Pallas kernels, on_device(): pl.pallas_call(functools.partial(kernel, n, snake, near_reach), out_shape...  32.4 us
    dot_general x1, matrix products, on_device(): return jnp.dot(mixed, w_output, preferred_element_type=f32).astype(bf)  3.67 us

profile of v4, /device:TPU:1, one launch (start us, length us, event | category | flops | bytes accessed | tf_op | source)
XLA Modules:
  0.0 36.1 jit_solution(7573024549136993860)
XLA Ops:
  0.0 0.0 copy-start
  0.0 32.4 %shard_map.73 = bf16[512,768]{1,0:T(8,128)(2,1)} custom-call(s32[32]{0:T(128)} %ft.1, f32[1536]{0:T(1024)} %gain.1, bf16[512,1536]{1,0:T(8,128)(2,1)} %x_hbm.1, bf16[1536,768]{1,0:T(8,128)(2,1)} %wq_hbm.1, bf16[1536,768]{1,0:T(8,128)(2,1)} %wk_hbm.1, bf16[1536,768]{1,0:T(8,128)(2,1)} %wv_hbm.1), custom_call_target="tpu_custom_call" | custom-call | tf_op jit(solution)/shard_map/pallas_call | solution.py:273
  32.4 0.0 copy-done
  32.4 3.7 %convolution_convert_fusion = bf16[512,1536]{1,0:T(8,128)(2,1)} fusion(bf16[512,768]{1,0:T(8,128)(2,1)} %shard_map.73, bf16[768,1536]{1,0:T(8,128)(2,1)S(1)} %copy-done), kind=kOutput, calls=%fused_computation | convolution fusion | flops 1208745984 | bytes 4718592 | tf_op jit(solution)/shard_map/dot_general | solution.py:304
Async XLA Ops:
  0.0 32.4 %copy-start = (bf16[768,1536]{1,0:T(8,128)(2,1)S(1)}, bf16[768,1536]{1,0:T(8,128)(2,1)}, u32[]{:S(2)}) copy-start(bf16[768,1536]{1,0:T(8,128)(2,1)} %param.13) | copy-start | bytes 7077892
